TPU v7x, 32 devices: a whole 2x2x4 slice. The times are simulated.
32 devices in a mesh: ep: 8 (over z, x), tp: 4 (over y, core).
Axes of the slice: x: 2, y: 2, z: 4, core: 2. Of those that a mesh axis runs over, the one named last changes fastest.
Arguments:
- hidden_in: bfloat16 [1024, 2048], P('ep', 'tp'), may hold values from -6 to 6
- norm_gain: float32 [2048], replicated, may hold values from 0.5 to 1.5
- router_weight: bfloat16 [2048, 8], replicated, may hold values from -4.861359 to 4.861359
- shared_gate_up: bfloat16 [2048, 2, 1408], P(None, None, 'tp'), may hold values from -0.125 to 0.125
- shared_down: bfloat16 [1408, 2048], P('tp'), may hold values from -0.15625 to 0.15625
- slot_gate_up: bfloat16 [32, 2048, 2, 704], P(('ep', 'tp')), as said below
- slot_down: bfloat16 [32, 704, 2048], P(('ep', 'tp')), as said below
- slot_expert: int32 [32], replicated, may hold values from 0 to 7, as said below
- slot_choice: int32 [1024, 6], P('ep'), may hold values from 0 to 31, all different within a row; in each aligned block of 32 rows (0 to 31, 32 to 63, ...) at most 12 rows name the same one
- live_count: int32 [8], P('ep'), may hold values from 64 to 128, as said below
Outputs:
- mixed_out: bfloat16 [1024, 2048], P('ep', 'tp')
Inputs may be any that keep to these rules, and one draw needn't show every extreme that they name: `slot_expert`: each expert is held by 1 or 7 slots; exactly 4 experts by the larger number. `slot_gate_up`: entry s holds the weights of expert slot_expert[s]; slots of one expert hold equal weights. `slot_down`: entry s holds the weights of expert slot_expert[s]; slots of one expert hold equal weights. `slot_choice`: a row names 6 different slots; in each aligned block of 32 rows no slot is named more than 12 times. `live_count`: the live rows of an index of ep are its first ones; some index of ep has all 128 rows live.
All inputs are finite; a program needn't handle non-finite values.
Results may differ from a plain program's by a relative error of at most 0.0058.
Values may be sent and summed in bfloat16 or wider, within the bound.
A program may use at most 64 MiB of HBM per device.

v0:
```python
import jax
import jax.numpy as jnp
from jax import lax
from jax.sharding import PartitionSpec as P


def gate_weights(normed_rows, choices, router_weight, slot_expert):
    logits = jnp.dot(normed_rows, router_weight, preferred_element_type=jnp.float32)
    slot_total = slot_expert.shape[0]
    expert_total = router_weight.shape[1]
    slot_hit = choices[:, :, None] == jnp.arange(slot_total, dtype=jnp.int32)
    expert_ids = jnp.sum(jnp.where(slot_hit, slot_expert, 0), axis=2)
    expert_hit = expert_ids[:, :, None] == jnp.arange(expert_total, dtype=jnp.int32)
    picked = jnp.sum(jnp.where(expert_hit, logits[:, None, :], 0.0), axis=2)
    highest = jnp.max(picked, axis=1, keepdims=True)
    weights = jnp.exp(picked - highest)
    return (weights / jnp.sum(weights, axis=1, keepdims=True)).astype(jnp.bfloat16)


def slot_positions(targets):
    length = targets.shape[0]
    same_slot = targets[:, None] == targets[None, :]
    earlier = jnp.arange(length)[None, :] < jnp.arange(length)[:, None]
    return jnp.sum(same_slot & earlier, axis=1)


def expert_apply(received, slot_gate_up, slot_down):
    shape_in = received.shape
    flat_rows = received.reshape(-1, shape_in[-1])
    gate_up = jnp.einsum(
        "rd,dgf->rgf", flat_rows, slot_gate_up[0], preferred_element_type=jnp.float32
    )
    activated = (jax.nn.silu(gate_up[:, 0]) * gate_up[:, 1]).astype(jnp.bfloat16)
    result = jnp.dot(activated, slot_down[0], preferred_element_type=jnp.float32).astype(
        jnp.bfloat16
    )
    return result.reshape(shape_in)


def local(
    hidden_in,
    norm_gain,
    router_weight,
    shared_gate_up,
    shared_down,
    slot_gate_up,
    slot_down,
    slot_expert,
    slot_choice,
    live_count,
):
    tp_count = lax.axis_size("tp")
    ep_count = lax.axis_size("ep")
    tp_index = lax.axis_index("tp")
    tok_count = hidden_in.shape[0]
    feature_width = hidden_in.shape[1] * tp_count
    top_count = slot_choice.shape[1]
    slot_count = slot_expert.shape[0]
    quarter = tok_count // tp_count
    capacity = max(2, 2 * quarter * top_count // slot_count)
    full_rows = lax.all_gather(hidden_in, "tp", axis=1, tiled=True)
    wide_rows = full_rows.astype(jnp.float32)
    norm_scale = lax.rsqrt(jnp.mean(wide_rows * wide_rows, axis=1, keepdims=True) + 1e-06)
    normed = (wide_rows * norm_scale * norm_gain).astype(jnp.bfloat16)
    shared_proj = jnp.einsum(
        "td,dgf->tgf", normed, shared_gate_up, preferred_element_type=jnp.float32
    )
    shared_hidden = (jax.nn.silu(shared_proj[:, 0]) * shared_proj[:, 1]).astype(jnp.bfloat16)
    partial_value = jnp.dot(shared_hidden, shared_down, preferred_element_type=jnp.float32)
    row_start = tp_index * quarter
    own_rows = lax.dynamic_slice_in_dim(normed, row_start, quarter, 0)
    own_choice = lax.dynamic_slice_in_dim(slot_choice, row_start, quarter, 0)
    gate_values = gate_weights(own_rows, own_choice, router_weight, slot_expert)
    targets = own_choice.reshape(-1)
    placed = targets * capacity + slot_positions(targets)
    outgoing = jnp.zeros((slot_count * capacity, feature_width), jnp.bfloat16)
    outgoing = outgoing.at[placed].set(jnp.repeat(own_rows, top_count, axis=0))
    outgoing = outgoing.reshape(ep_count, tp_count, capacity, feature_width)
    arrived = lax.all_to_all(
        lax.all_to_all(outgoing, "ep", split_axis=0, concat_axis=0, tiled=True),
        "tp",
        split_axis=1,
        concat_axis=1,
        tiled=True,
    )
    computed = expert_apply(arrived, slot_gate_up, slot_down)
    returned = lax.all_to_all(
        lax.all_to_all(computed, "ep", split_axis=0, concat_axis=0, tiled=True),
        "tp",
        split_axis=1,
        concat_axis=1,
        tiled=True,
    )
    fetched = returned.reshape(-1, feature_width)[placed].reshape(quarter, top_count, feature_width)
    routed = jnp.einsum("qk,qkd->qd", gate_values, fetched, preferred_element_type=jnp.float32)
    own_partial = lax.dynamic_slice_in_dim(partial_value, row_start, quarter, 0) + routed
    partial_value = lax.dynamic_update_slice_in_dim(partial_value, own_partial, row_start, 0)
    summed = lax.psum_scatter(partial_value, "tp", scatter_dimension=1, tiled=True)
    live_rows = jnp.arange(tok_count, dtype=jnp.int32) < live_count[0]
    mixed_out = jnp.where(live_rows[:, None], hidden_in.astype(jnp.float32) + summed, 0.0)
    return mixed_out.astype(jnp.bfloat16)


def solution(mesh):
    in_specs = (
        P("ep", "tp"),
        P(),
        P(),
        P(None, None, "tp"),
        P("tp", None),
        P(("ep", "tp"), None, None, None),
        P(("ep", "tp"), None, None),
        P(),
        P("ep", None),
        P("ep"),
    )
    out_specs = P("ep", "tp")
    return jax.shard_map(local, mesh=mesh, in_specs=in_specs, out_specs=out_specs, check_vma=False)
```

profile of v0, /device:TPU:0, one launch (start us, length us, event | category | flops | bytes accessed | tf_op | source)
XLA Modules:
  0.0 238.2 jit_solution(8258291260687447549)
XLA Ops:
  6.5 9.0 %all_gather.3 = bf16[128,2048]{1,0:T(8,128)(2,1)S(1)} all-gather(bf16[128,512]{1,0:T(8,128)(2,1)} %param.10), channel_id=1, replica_groups=mesh['ep'=8,'tp'=4] {'tp'}, dimensions={1}, use_global_device_ids=true | all-gather | bytes 655360 | tf_op jit(solution)/shard_map/all_gather | solution.py:61
  19.2 2.2 reshape.86
  21.4 3.7 %scatter_custom_fusion = bf16[384,2048]{1,0:T(8,128)(2,1)} fusion(s32[192]{0:T(256)S(1)} %bitcast.43, bf16[192,2048]{1,0:T(8,128)(2,1)} %reshape.86, bf16[]{:T(256)} %constant.10.clone.1), kind=kCustom, calls=%fused_computation.14 | custom fusion | bytes 1573376 | tf_op jit(solution)/shard_map/scatter | solution.py:77
  25.1 3.6 %reshape.69 = bf16[8,4,12,2048]{3,2,1,0:T(8,128)(2,1)} reshape(bf16[384,2048]{1,0:T(8,128)(2,1)} %scatter_custom_fusion) | data formatting | bytes 3145728 | tf_op jit(solution)/shard_map/reshape | solution.py:78
  28.7 2.8 %copy.29 = bf16[8,4,12,2048]{3,1,2,0:T(4,128)(2,1)S(1)} copy(bf16[8,4,12,2048]{3,2,1,0:T(8,128)(2,1)} %reshape.69) | data formatting | bytes 3145728 | tf_op jit(solution)/shard_map/reshape | solution.py:78
  31.5 43.1 %all_to_all.20 = bf16[8,4,12,2048]{3,1,2,0:T(4,128)(2,1)S(1)} all-to-all(bf16[8,4,12,2048]{3,1,2,0:T(4,128)(2,1)S(1)} %copy.29), channel_id=1, replica_groups=mesh['ep'=8,'tp'=4] {'ep'}, dimensions={0} | all-to-all | bytes 3145728 | tf_op jit(solution)/shard_map/all_to_all | solution.py:80
  75.5 22.5 %all_to_all.21 = bf16[8,4,12,2048]{3,0,2,1:T(8,128)(2,1)S(1)} all-to-all(bf16[8,4,12,2048]{3,0,2,1:T(8,128)(2,1)S(1)} %copy.30), channel_id=1, replica_groups=mesh['ep'=8,'tp'=4] {'tp'}, dimensions={1} | all-to-all | bytes 3145728 | tf_op jit(solution)/shard_map/all_to_all | solution.py:79
  98.0 2.2 copy.31
  100.3 3.6 %reshape.91 = bf16[384,2048,1]{1,0,2:T(8,128)(2,1)} reshape(bf16[8,4,12,2048]{3,2,1,0:T(8,128)(2,1)} %copy.31) | data formatting | bytes 3145728 | tf_op jit(solution)/shard_map/reshape | solution.py:29
  103.9 5.6 %fusion = f32[384,2,704]{0,2,1:T(8,128)S(1)} fusion(bf16[384,2048,1]{1,0,2:T(8,128)(2,1)} %reshape.91, bf16[1,2048,2,704]{1,3,2,0:T(8,128)(2,1)} %param.15), kind=kOutput, calls=%fused_computation.2 | convolution fusion | flops 2214592512 | bytes 9502720 | tf_op jit(solution)/shard_map/rd,dgf->rgf/dot_general | solution.py:30
  109.5 2.6 %fusion.4 = bf16[384,2048]{1,0:T(8,128)(2,1)} fusion(bf16[1,704,2048]{2,1,0:T(8,128)(2,1)S(1)} %copy-done, f32[384,2,704]{0,2,1:T(8,128)S(1)} %fusion), kind=kOutput, calls=%fused_computation.6 | convolution fusion | flops 1109704704 | bytes 6619136 | tf_op jit(solution)/shard_map/dot_general | solution.py:34
  112.2 3.6 %reshape.71 = bf16[8,4,12,2048]{3,2,1,0:T(8,128)(2,1)} reshape(bf16[384,2048]{1,0:T(8,128)(2,1)} %fusion.4) | data formatting | bytes 3145728 | tf_op jit(solution)/shard_map/reshape | solution.py:37
  115.8 4.0 %copy.32 = bf16[8,4,12,2048]{3,1,2,0:T(4,128)(2,1)} copy(bf16[8,4,12,2048]{3,2,1,0:T(8,128)(2,1)} %reshape.71) | data formatting | bytes 3145728 | tf_op jit(solution)/shard_map/reshape | solution.py:37
  119.7 4.6 %all-to-all-start.2 = ((bf16[8,4,12,2048]{3,1,2,0:T(4,128)(2,1)}), bf16[8,4,12,2048]{3,1,2,0:T(4,128)(2,1)}, u32[]{:S(2)}, u32[]{:S(2)}) async-start(bf16[8,4,12,2048]{3,1,2,0:T(4,128)(2,1)} %copy.32), calls=%async_computation.2 | async-start | bytes 3145728 | tf_op jit(solution)/shard_map/all_to_all | solution.py:88
  124.5 36.6 %all-to-all-done.2 = bf16[8,4,12,2048]{3,1,2,0:T(4,128)(2,1)} async-done(((bf16[8,4,12,2048]{3,1,2,0:T(4,128)(2,1)}), bf16[8,4,12,2048]{3,1,2,0:T(4,128)(2,1)}, u32[]{:S(2)}, u32[]{:S(2)}) %all-to-all-start.2) | async-done | bytes 1572896 | tf_op jit(solution)/shard_map/all_to_all | solution.py:88
  161.1 3.4 %copy.33 = bf16[8,4,12,2048]{3,0,2,1:T(8,128)(2,1)} copy(bf16[8,4,12,2048]{3,1,2,0:T(4,128)(2,1)} %all-to-all-done.2) | data formatting | bytes 3145728 | tf_op jit(solution)/shard_map/all_to_all | solution.py:88
  164.5 4.5 %all-to-all-start.3 = ((bf16[8,4,12,2048]{3,0,2,1:T(8,128)(2,1)}), bf16[8,4,12,2048]{3,0,2,1:T(8,128)(2,1)}, u32[]{:S(2)}, u32[]{:S(2)}) async-start(bf16[8,4,12,2048]{3,0,2,1:T(8,128)(2,1)} %copy.33), calls=%async_computation.3 | async-start | bytes 3145728 | tf_op jit(solution)/shard_map/all_to_all | solution.py:87
  169.5 2.8 %fusion.15 = f32[128,2,352]{0,2,1:T(8,128)S(1)} fusion(bf16[2048,2,352]{0,2,1:T(8,128)(2,1)} %param.13, bf16[128,2048]{1,0:T(8,128)(2,1)S(1)} %copy-done.2), kind=kOutput, calls=%fused_computation.17 | convolution fusion | flops 369098752 | bytes 3768320 | tf_op jit(solution)/shard_map/td,dgf->tgf/dot_general | solution.py:65
  173.9 15.2 %all-to-all-done.3 = bf16[8,4,12,2048]{3,0,2,1:T(8,128)(2,1)} async-done(((bf16[8,4,12,2048]{3,0,2,1:T(8,128)(2,1)}), bf16[8,4,12,2048]{3,0,2,1:T(8,128)(2,1)}, u32[]{:S(2)}, u32[]{:S(2)}) %all-to-all-start.3) | async-done | bytes 1572896 | tf_op jit(solution)/shard_map/all_to_all | solution.py:87
  189.1 3.6 %copy.34 = bf16[8,4,12,2048]{3,2,1,0:T(8,128)(2,1)} copy(bf16[8,4,12,2048]{3,0,2,1:T(8,128)(2,1)} %all-to-all-done.3) | data formatting | bytes 3145728 | tf_op jit(solution)/shard_map/all_to_all | solution.py:87
  192.8 3.6 %reshape.72 = bf16[384,2048]{1,0:T(8,128)(2,1)} reshape(bf16[8,4,12,2048]{3,2,1,0:T(8,128)(2,1)} %copy.34) | data formatting | bytes 3145728 | tf_op jit(solution)/shard_map/reshape | solution.py:94
  196.4 4.4 %gather_fusion = bf16[192,2048]{1,0:T(8,128)(2,1)} fusion(bf16[384,2048]{1,0:T(8,128)(2,1)} %reshape.72, s32[1024]{0:T(1024)S(1)} %pad_clamp_fusion), kind=kCustom, calls=%fused_computation | custom fusion | bytes 1573632 | tf_op jit(solution)/shard_map/gather | solution.py:94
  200.8 2.2 reshape.73
  207.1 22.5 %reduce-scatter.2.cloned.1.call-done = f32[128,512]{1,0:T(8,128)} async-done(((f32[128,2048]{1,0:T(8,128)}), f32[128,512]{1,0:T(8,128)}) %reduce-scatter.2.cloned.1.call-update) | async-done | bytes 262160 | tf_op jit(solution)/shard_map/reduce_scatter | solution.py:98
  (44 shorter events, 11.8 us)
Async XLA Ops:
  6.5 103.0 %copy-start = (bf16[1,704,2048]{2,1,0:T(8,128)(2,1)S(1)}, bf16[1,704,2048]{2,1,0:T(8,128)(2,1)}, u32[]{:S(2)}) copy-start(bf16[1,704,2048]{2,1,0:T(8,128)(2,1)} %param.16) | copy-start | bytes 8650756
  6.5 10.9 %copy-start.6 = (s32[128,6]{0,1:T(8,128)S(1)}, s32[128,6]{0,1:T(8,128)}, u32[]{:S(2)}) copy-start(s32[128,6]{0,1:T(8,128)} %param.18) | copy-start | bytes 9220
  16.6 0.8 copy-start.1
  119.7 4.6 %copy-start.5 = (bf16[2048,8]{0,1:T(8,128)(2,1)S(1)}, bf16[2048,8]{0,1:T(8,128)(2,1)}, u32[]{:S(2)}) copy-start(bf16[2048,8]{0,1:T(8,128)(2,1)} %param.12) | copy-start | bytes 98308
  119.7 41.3 %all-to-all-start.2 = ((bf16[8,4,12,2048]{3,1,2,0:T(4,128)(2,1)}), bf16[8,4,12,2048]{3,1,2,0:T(4,128)(2,1)}, u32[]{:S(2)}, u32[]{:S(2)}) async-start(bf16[8,4,12,2048]{3,1,2,0:T(4,128)(2,1)} %copy.32), calls=%async_computation.2 | async-start | bytes 3145728 | tf_op jit(solution)/shard_map/all_to_all | solution.py:88
  164.5 4.5 %copy-start.7 = (s32[32]{0:T(128)S(1)}, s32[32]{0:T(128)}, u32[]{:S(2)}) copy-start(s32[32]{0:T(128)} %param.17) | copy-start | bytes 388
  164.5 5.0 %copy-start.2 = (bf16[128,2048]{1,0:T(8,128)(2,1)S(1)}, bf16[128,2048]{1,0:T(8,128)(2,1)}, u32[]{:S(2)}) copy-start(bf16[128,2048]{1,0:T(8,128)(2,1)} %copy-done.1) | copy-start | bytes 1572868
  164.5 24.6 %all-to-all-start.3 = ((bf16[8,4,12,2048]{3,0,2,1:T(8,128)(2,1)}), bf16[8,4,12,2048]{3,0,2,1:T(8,128)(2,1)}, u32[]{:S(2)}, u32[]{:S(2)}) async-start(bf16[8,4,12,2048]{3,0,2,1:T(8,128)(2,1)} %copy.33), calls=%async_computation.3 | async-start | bytes 3145728 | tf_op jit(solution)/shard_map/all_to_all | solution.py:87
  169.0 60.6 %reduce-scatter.2.cloned.1.call-start = ((), (), s32[]{:S(2)}) async-start(), calls=%async_computation.5 | async-start | bytes 1310720 | tf_op jit(solution)/shard_map/reduce_scatter | solution.py:98
  169.5 2.9 %copy-start.3 = (bf16[352,2048]{1,0:T(8,128)(2,1)S(1)}, bf16[352,2048]{1,0:T(8,128)(2,1)}, u32[]{:S(2)}) copy-start(bf16[352,2048]{1,0:T(8,128)(2,1)} %param.14) | copy-start | bytes 4325380
  203.0 26.6 %copy-start.4 = (bf16[128,512]{1,0:T(8,128)(2,1)S(1)}, bf16[128,512]{1,0:T(8,128)(2,1)}, u32[]{:S(2)}) copy-start(bf16[128,512]{1,0:T(8,128)(2,1)} %param.10) | copy-start | bytes 393220
Sparse Core Ops, SparseCore 0:
  206.6 22.9 reduce-scatter.1
where the time goes:
time: 239 us; the launch traced here: 238 us
  blocking collectives  74.6 us (31%)
  waiting for transfers between devices  74.3 us (31%)
  local copies, waits for them, and re-layouts  46.3 us (19%)
  matrix products  14.5 us (6%)
  between operations  14.2 us (6%)
  starting transfers between devices  9.12 us (4%)
  other arithmetic  5.13 us (2%)
    all_to_all x1, blocking collectives, local(): lax.all_to_all(outgoing, 'ep', split_axis=0, concat_axis=0, tiled=True)  43.1 us
    all_to_all x1, waiting for transfers between devices, local(): lax.all_to_all(computed, 'ep', split_axis=0, concat_axis=0, tiled=True)  36.6 us
    all_to_all x1, blocking collectives, local(): lax.all_to_all(lax.all_to_all(outgoing, 'ep', split_axis=0, concat_axis=0...  22.5 us
    reduce_scatter x1, waiting for transfers between devices, local(): lax.psum_scatter(partial_value, 'tp', scatter_dimension=1, tiled=True)  22.5 us
    all_to_all x1, waiting for transfers between devices, local(): lax.all_to_all(lax.all_to_all(computed, 'ep', split_axis=0, concat_axis=0...  15.2 us
    all_gather x1, blocking collectives, local(): full_rows = lax.all_gather(hidden_in, 'tp', axis=1, tiled=True)  8.98 us
    reshape x2, local copies, waits for them, and re-layouts, expert_apply(): return result.reshape(shape_in)  7.55 us
    reshape x2, local copies, waits for them, and re-layouts, local(): outgoing = outgoing.reshape(ep_count, tp_count, capacity, feature_width)  6.42 us
  transfers between devices with their start and end apart: 3, of which 3 were waited for; matrix products, arithmetic and copies ran while one was open for 2% of the time, Pallas kernels for 0%

commit v1 on v0

--- a/solution.py
+++ b/solution.py
@@ -76,12 +76,20 @@
     outgoing = jnp.zeros((slot_count * capacity, feature_width), jnp.bfloat16)
     outgoing = outgoing.at[placed].set(jnp.repeat(own_rows, top_count, axis=0))
     outgoing = outgoing.reshape(ep_count, tp_count, capacity, feature_width)
-    arrived = lax.all_to_all(
-        lax.all_to_all(outgoing, "ep", split_axis=0, concat_axis=0, tiled=True),
-        "tp",
-        split_axis=1,
-        concat_axis=1,
-        tiled=True,
+    arrived = jnp.concatenate(
+        lax.all_to_all(
+            jnp.stack(
+                jnp.split(
+                    lax.all_to_all(outgoing, "ep", split_axis=0, concat_axis=0, tiled=True),
+                    lax.axis_size("tp"),
+                    axis=1,
+                )
+            ),
+            "tp",
+            0,
+            0,
+        ),
+        axis=1,
     )
     computed = expert_apply(arrived, slot_gate_up, slot_down)
     returned = lax.all_to_all(

time: 239 us -> 243 us (1.017)
  local copies, waits for them, and re-layouts: 46.3 us -> 49.3 us
    another operation x0 -> x3, local copies, waits for them, and re-layouts: none -> 5.3 us  [the longest x1 3.61 us: expert_apply(): flat_rows = received.reshape(-1, shape_in[-1])]
    all_to_all x2 -> x0, local copies, waits for them, and re-layouts: 3.1 us -> none  [the longest x1 2.24 us: local(): lax.all_to_all(lax.all_to_all(outgoing, 'ep', split_axis=0, concat_axis=0...]
    split x0 -> x1, local copies, waits for them, and re-layouts: none -> 2.92 us  [local(): jnp.split(lax.all_to_all(outgoing, 'ep', split_axis=0, concat_axis=0, til...]
where the time goes in v1:
time: 243 us; the launch traced here: 242 us
  blocking collectives  74.5 us (31%)
  waiting for transfers between devices  73.8 us (30%)
  local copies, waits for them, and re-layouts  49.3 us (20%)
  matrix products  15.2 us (6%)
  between operations  14.2 us (6%)
  starting transfers between devices  8.82 us (4%)
  other arithmetic  6.16 us (3%)
    all_to_all x1, blocking collectives, local(): lax.all_to_all(outgoing, 'ep', split_axis=0, concat_axis=0, tiled=True)  43.1 us
    all_to_all x1, waiting for transfers between devices, local(): lax.all_to_all(computed, 'ep', split_axis=0, concat_axis=0, tiled=True)  36 us
    all_to_all x1, blocking collectives, local(): lax.all_to_all(jnp.stack(jnp.split(lax.all_to_all(outgoing, 'ep', split_a...  22.5 us
    reduce_scatter x1, waiting for transfers between devices, local(): lax.psum_scatter(partial_value, 'tp', scatter_dimension=1, tiled=True)  22.5 us
    all_to_all x1, waiting for transfers between devices, local(): lax.all_to_all(lax.all_to_all(computed, 'ep', split_axis=0, concat_axis=0...  15.3 us
    all_gather x1, blocking collectives, local(): full_rows = lax.all_gather(hidden_in, 'tp', axis=1, tiled=True)  8.86 us
    reshape x2, local copies, waits for them, and re-layouts, expert_apply(): return result.reshape(shape_in)  7.57 us
    reshape x2, local copies, waits for them, and re-layouts, local(): outgoing = outgoing.reshape(ep_count, tp_count, capacity, feature_width)  6.43 us
  transfers between devices with their start and end apart: 3, of which 3 were waited for; matrix products, arithmetic and copies ran while one was open for 2% of the time, Pallas kernels for 0%

profile of v1, /device:TPU:0, one launch (start us, length us, event | category | flops | bytes accessed | tf_op | source)
XLA Modules:
  0.0 242.0 jit_solution(12542555993099882972)
XLA Ops:
  8.0 8.9 %all_gather.3 = bf16[128,2048]{1,0:T(8,128)(2,1)S(1)} all-gather(bf16[128,512]{1,0:T(8,128)(2,1)} %param.10), channel_id=1, replica_groups=mesh['ep'=8,'tp'=4] {'tp'}, dimensions={1}, use_global_device_ids=true | all-gather | bytes 655360 | tf_op jit(solution)/shard_map/all_gather | solution.py:61
  21.3 3.7 %scatter_custom_fusion = bf16[384,2048]{1,0:T(8,128)(2,1)} fusion(s32[192]{0:T(256)S(1)} %bitcast.55, bf16[192,2048]{1,0:T(8,128)(2,1)} %reshape.86, bf16[]{:T(256)} %constant.10.clone.1), kind=kCustom, calls=%fused_computation.15 | custom fusion | bytes 1573376 | tf_op jit(solution)/shard_map/scatter | solution.py:77
  25.0 3.6 %reshape.69 = bf16[8,4,12,2048]{3,2,1,0:T(8,128)(2,1)} reshape(bf16[384,2048]{1,0:T(8,128)(2,1)} %scatter_custom_fusion) | data formatting | bytes 3145728 | tf_op jit(solution)/shard_map/reshape | solution.py:78
  28.6 2.8 %copy.52 = bf16[8,4,12,2048]{3,1,2,0:T(4,128)(2,1)S(1)} copy(bf16[8,4,12,2048]{3,2,1,0:T(8,128)(2,1)} %reshape.69) | data formatting | bytes 3145728 | tf_op jit(solution)/shard_map/reshape | solution.py:78
  31.5 43.1 %all_to_all.20 = bf16[8,4,12,2048]{3,1,2,0:T(4,128)(2,1)S(1)} all-to-all(bf16[8,4,12,2048]{3,1,2,0:T(4,128)(2,1)S(1)} %copy.52), channel_id=1, replica_groups=mesh['ep'=8,'tp'=4] {'ep'}, dimensions={0} | all-to-all | bytes 3145728 | tf_op jit(solution)/shard_map/all_to_all | solution.py:83
  74.5 2.9 %fusion.28 = (bf16[8,1,12,2048]{3,1,2,0:T(2,128)(2,1)S(1)}, bf16[8,1,12,2048]{3,1,2,0:T(2,128)(2,1)S(1)}, bf16[8,1,12,2048]{3,1,2,0:T(2,128)(2,1)S(1)}, bf16[8,1,12,2048]{3,1,2,0:T(2,128)(2,1)S(1)}) fusion(bf16[8,4,12,2048]{3,1,2,0:T(4,128)(2,1)S(1)} %all_to_all.20), kind=kLoop, calls=%fused_computation.53 | loop fusion | bytes 3145728 | tf_op jit(solution)/shard_map/split | solution.py:82
  79.4 22.5 %all_to_all.21 = bf16[4,8,1,12,2048]{4,1,3,2,0:T(8,128)(2,1)S(1)} all-to-all(bf16[4,8,1,12,2048]{4,1,3,2,0:T(8,128)(2,1)S(1)} %pad_maximum_fusion), channel_id=1, replica_groups=mesh['ep'=8,'tp'=4] {'tp'}, dimensions={0} | all-to-all | bytes 3145728 | tf_op jit(solution)/shard_map/all_to_all | solution.py:80
  101.9 2.2 copy.57
  104.1 3.6 %reshape.91 = bf16[384,2048,1]{1,0,2:T(8,128)(2,1)} reshape(bf16[8,4,1,12,2048]{4,3,1,0,2:T(8,128)(2,1)} %copy.57) | data formatting | bytes 3145728 | tf_op jit(solution)/shard_map/reshape;reshape | solution.py:29
  107.7 5.6 %fusion = f32[384,2,704]{0,2,1:T(8,128)S(1)} fusion(bf16[384,2048,1]{1,0,2:T(8,128)(2,1)} %reshape.91, bf16[1,2048,2,704]{1,3,2,0:T(8,128)(2,1)} %param.15), kind=kOutput, calls=%fused_computation.2 | convolution fusion | flops 2214592512 | bytes 9502720 | tf_op jit(solution)/shard_map/rd,dgf->rgf/dot_general | solution.py:30
  113.4 2.7 %fusion.4 = bf16[384,2048]{1,0:T(8,128)(2,1)} fusion(bf16[1,704,2048]{2,1,0:T(8,128)(2,1)S(1)} %copy-done, f32[384,2,704]{0,2,1:T(8,128)S(1)} %fusion), kind=kOutput, calls=%fused_computation.6 | convolution fusion | flops 1109704704 | bytes 6619136 | tf_op jit(solution)/shard_map/dot_general | solution.py:34
  116.1 3.6 %reshape.71 = bf16[8,4,12,2048]{3,2,1,0:T(8,128)(2,1)} reshape(bf16[384,2048]{1,0:T(8,128)(2,1)} %fusion.4) | data formatting | bytes 3145728 | tf_op jit(solution)/shard_map/reshape | solution.py:37
  119.7 4.0 %copy.58 = bf16[8,4,12,2048]{3,1,2,0:T(4,128)(2,1)} copy(bf16[8,4,12,2048]{3,2,1,0:T(8,128)(2,1)} %reshape.71) | data formatting | bytes 3145728 | tf_op jit(solution)/shard_map/reshape | solution.py:37
  123.6 4.3 %all-to-all-start.2 = ((bf16[8,4,12,2048]{3,1,2,0:T(4,128)(2,1)}), bf16[8,4,12,2048]{3,1,2,0:T(4,128)(2,1)}, u32[]{:S(2)}, u32[]{:S(2)}) async-start(bf16[8,4,12,2048]{3,1,2,0:T(4,128)(2,1)} %copy.58), calls=%async_computation.2 | async-start | bytes 3145728 | tf_op jit(solution)/shard_map/all_to_all | solution.py:96
  128.8 36.0 %all-to-all-done.2 = bf16[8,4,12,2048]{3,1,2,0:T(4,128)(2,1)} async-done(((bf16[8,4,12,2048]{3,1,2,0:T(4,128)(2,1)}), bf16[8,4,12,2048]{3,1,2,0:T(4,128)(2,1)}, u32[]{:S(2)}, u32[]{:S(2)}) %all-to-all-start.2) | async-done | bytes 1572896 | tf_op jit(solution)/shard_map/all_to_all | solution.py:96
  164.9 3.4 %copy.59 = bf16[8,4,12,2048]{3,0,2,1:T(8,128)(2,1)} copy(bf16[8,4,12,2048]{3,1,2,0:T(4,128)(2,1)} %all-to-all-done.2) | data formatting | bytes 3145728 | tf_op jit(solution)/shard_map/all_to_all | solution.py:96
  168.3 4.5 %all-to-all-start.3 = ((bf16[8,4,12,2048]{3,0,2,1:T(8,128)(2,1)}), bf16[8,4,12,2048]{3,0,2,1:T(8,128)(2,1)}, u32[]{:S(2)}, u32[]{:S(2)}) async-start(bf16[8,4,12,2048]{3,0,2,1:T(8,128)(2,1)} %copy.59), calls=%async_computation.3 | async-start | bytes 3145728 | tf_op jit(solution)/shard_map/all_to_all | solution.py:95
  173.3 2.8 %fusion.15 = f32[128,2,352]{0,2,1:T(8,128)S(1)} fusion(bf16[2048,2,352]{0,2,1:T(8,128)(2,1)} %param.13, bf16[128,2048]{1,0:T(8,128)(2,1)S(1)} %fusion.10), kind=kOutput, calls=%fused_computation.18 | convolution fusion | flops 369098752 | bytes 3768320 | tf_op jit(solution)/shard_map/td,dgf->tgf/dot_general | solution.py:65
  177.6 15.3 %all-to-all-done.3 = bf16[8,4,12,2048]{3,0,2,1:T(8,128)(2,1)} async-done(((bf16[8,4,12,2048]{3,0,2,1:T(8,128)(2,1)}), bf16[8,4,12,2048]{3,0,2,1:T(8,128)(2,1)}, u32[]{:S(2)}, u32[]{:S(2)}) %all-to-all-start.3) | async-done | bytes 1572896 | tf_op jit(solution)/shard_map/all_to_all | solution.py:95
  192.9 3.7 %copy.60 = bf16[8,4,12,2048]{3,2,1,0:T(8,128)(2,1)} copy(bf16[8,4,12,2048]{3,0,2,1:T(8,128)(2,1)} %all-to-all-done.3) | data formatting | bytes 3145728 | tf_op jit(solution)/shard_map/all_to_all | solution.py:95
  196.6 3.6 %reshape.72 = bf16[384,2048]{1,0:T(8,128)(2,1)} reshape(bf16[8,4,12,2048]{3,2,1,0:T(8,128)(2,1)} %copy.60) | data formatting | bytes 3145728 | tf_op jit(solution)/shard_map/reshape | solution.py:102
  200.2 4.4 %gather_fusion = bf16[192,2048]{1,0:T(8,128)(2,1)} fusion(bf16[384,2048]{1,0:T(8,128)(2,1)} %reshape.72, s32[1024]{0:T(1024)S(1)} %pad_clamp_fusion), kind=kCustom, calls=%fused_computation | custom fusion | bytes 1573632 | tf_op jit(solution)/shard_map/gather | solution.py:102
  204.6 2.2 reshape.73
  210.9 22.5 %reduce-scatter.2.cloned.1.call-done = f32[128,512]{1,0:T(8,128)} async-done(((f32[128,2048]{1,0:T(8,128)}), f32[128,512]{1,0:T(8,128)}) %reduce-scatter.2.cloned.1.call-update) | async-done | bytes 262160 | tf_op jit(solution)/shard_map/reduce_scatter | solution.py:106
  (39 shorter events, 15.8 us)
Async XLA Ops:
  6.5 106.9 %copy-start = (bf16[1,704,2048]{2,1,0:T(8,128)(2,1)S(1)}, bf16[1,704,2048]{2,1,0:T(8,128)(2,1)}, u32[]{:S(2)}) copy-start(bf16[1,704,2048]{2,1,0:T(8,128)(2,1)} %param.16) | copy-start | bytes 8650756
  123.6 41.2 %all-to-all-start.2 = ((bf16[8,4,12,2048]{3,1,2,0:T(4,128)(2,1)}), bf16[8,4,12,2048]{3,1,2,0:T(4,128)(2,1)}, u32[]{:S(2)}, u32[]{:S(2)}) async-start(bf16[8,4,12,2048]{3,1,2,0:T(4,128)(2,1)} %copy.58), calls=%async_computation.2 | async-start | bytes 3145728 | tf_op jit(solution)/shard_map/all_to_all | solution.py:96
  168.3 4.6 %copy-start.3 = (s32[32]{0:T(128)S(1)}, s32[32]{0:T(128)}, u32[]{:S(2)}) copy-start(s32[32]{0:T(128)} %param.17) | copy-start | bytes 388
  168.3 24.6 %all-to-all-start.3 = ((bf16[8,4,12,2048]{3,0,2,1:T(8,128)(2,1)}), bf16[8,4,12,2048]{3,0,2,1:T(8,128)(2,1)}, u32[]{:S(2)}, u32[]{:S(2)}) async-start(bf16[8,4,12,2048]{3,0,2,1:T(8,128)(2,1)} %copy.59), calls=%async_computation.3 | async-start | bytes 3145728 | tf_op jit(solution)/shard_map/all_to_all | solution.py:95
  172.8 60.7 %reduce-scatter.2.cloned.1.call-start = ((), (), s32[]{:S(2)}) async-start(), calls=%async_computation.5 | async-start | bytes 1310720 | tf_op jit(solution)/shard_map/reduce_scatter | solution.py:106
  173.3 2.9 %copy-start.1 = (bf16[352,2048]{1,0:T(8,128)(2,1)S(1)}, bf16[352,2048]{1,0:T(8,128)(2,1)}, u32[]{:S(2)}) copy-start(bf16[352,2048]{1,0:T(8,128)(2,1)} %param.14) | copy-start | bytes 4325380
  206.8 26.6 %copy-start.2 = (bf16[128,512]{1,0:T(8,128)(2,1)S(1)}, bf16[128,512]{1,0:T(8,128)(2,1)}, u32[]{:S(2)}) copy-start(bf16[128,512]{1,0:T(8,128)(2,1)} %param.10) | copy-start | bytes 393220
Sparse Core Ops, SparseCore 0:
  210.4 23.0 reduce-scatter.1
